TPU v7x, 256 devices: a whole 4x4x8 slice. The times are simulated.
256 devices in a mesh: space: 32 (over z, x_lo, core), filt: 8 (over y, x_hi).
Axes of the slice: x: 4 (x_hi: 2, x_lo: 2; x = x_hi * 2 + x_lo), y: 4, z: 8, core: 2. Of those that a mesh axis runs over, the one named last changes fastest.
Arguments:
- volume: bfloat16 [64, 128, 32, 128], P('space', 'filt'), may hold values from -6 to 6
- kernel: bfloat16 [3, 3, 3, 256, 128], P(None, None, None, 'filt'), may hold values from -0.109375 to 0.109375
- out_grad: bfloat16 [32, 64, 16, 256], P('space', None, None, 'filt'), may hold values from -6 to 6
Outputs:
- features: bfloat16 [32, 64, 16, 256], P('space', None, None, 'filt')
- in_grad: bfloat16 [64, 128, 32, 128], P('space', 'filt')
- kernel_grad: float32 [3, 3, 3, 256, 128], P(None, None, None, 'filt')
All inputs are finite; a program needn't handle non-finite values.
Results may differ from a plain program's by a relative error of at most 0.001.
Values may be sent and summed in bfloat16 or wider, within the bound.
A program may use at most 64 MiB of HBM per device.

v0:
```python
import jax
import jax.numpy as jnp
from jax import lax
from jax.sharding import PartitionSpec as P


def from_behind(shard, axis, by):
    peers = lax.axis_size(axis)
    pairs = [(i, i + by) for i in range(peers) if 0 <= i + by < peers]
    return lax.ppermute(shard, axis, pairs)


def take_patch(padded, a, b, c, dims):
    ox, oy, oz = dims
    chan = padded.shape[3]
    return lax.slice(
        padded, (a, b, c, 0), (a + 2 * ox - 1, b + 2 * oy - 1, c + 2 * oz - 1, chan), (2, 2, 2, 1)
    )


def conv_out(padded, weights, dims):
    chan = padded.shape[3]
    total = jnp.zeros((dims[0] * dims[1] * dims[2], weights.shape[3]), jnp.float32)
    for a in range(3):
        for b in range(3):
            for c in range(3):
                patch = take_patch(padded, a, b, c, dims).reshape(-1, chan)
                total = total + lax.dot_general(
                    patch,
                    weights[a, b, c],
                    (((1,), (1,)), ((), ())),
                    preferred_element_type=jnp.float32,
                )
    return total


def weight_terms(padded, grad_rows, dims):
    chan = padded.shape[3]
    pieces = []
    for a in range(3):
        for b in range(3):
            for c in range(3):
                patch = take_patch(padded, a, b, c, dims).reshape(-1, chan)
                pieces.append(
                    lax.dot_general(
                        grad_rows,
                        patch,
                        (((0,), (0,)), ((), ())),
                        preferred_element_type=jnp.float32,
                    )
                )
    return jnp.stack(pieces).reshape(3, 3, 3, grad_rows.shape[1], chan)


def parity_transpose(grad_window, weights):
    extent_x, extent_y, extent_z, channels_out = grad_window.shape
    channels_in = weights.shape[4]
    grad_padded = jnp.pad(grad_window, ((1, 1), (1, 1), (1, 1), (0, 0)))
    tap_table = (((0, 1), (2, 0)), ((1, 1),))
    shape_out = (extent_x + 1, extent_y + 1, extent_z + 1)
    plane_list = []
    for parity_x in range(2):
        row_list = []
        for parity_y in range(2):
            depth_list = []
            for parity_z in range(2):
                summed = jnp.zeros(
                    (shape_out[0] * shape_out[1] * shape_out[2], channels_in), jnp.float32
                )
                for a, shift_x in tap_table[parity_x]:
                    for b, shift_y in tap_table[parity_y]:
                        for c, shift_z in tap_table[parity_z]:
                            window_piece = lax.slice(
                                grad_padded,
                                (shift_x, shift_y, shift_z, 0),
                                (
                                    shift_x + shape_out[0],
                                    shift_y + shape_out[1],
                                    shift_z + shape_out[2],
                                    channels_out,
                                ),
                            ).reshape(-1, channels_out)
                            summed = summed + jnp.dot(
                                window_piece, weights[a, b, c], preferred_element_type=jnp.float32
                            )
                depth_list.append(
                    summed.reshape(shape_out[0], shape_out[1], shape_out[2], channels_in)
                )
            joined = jnp.stack(depth_list, axis=3).reshape(
                shape_out[0], shape_out[1], 2 * shape_out[2], channels_in
            )
            row_list.append(joined)
        joined = jnp.stack(row_list, axis=2).reshape(
            shape_out[0], 2 * shape_out[1], 2 * shape_out[2], channels_in
        )
        plane_list.append(joined)
    return jnp.stack(plane_list, axis=1).reshape(
        2 * shape_out[0], 2 * shape_out[1], 2 * shape_out[2], channels_in
    )


def on_device(volume, kernel, out_grad):
    planes, rows, depth, cin = volume.shape
    grad_all, kern_all = (
        lax.all_gather(out_grad, "filt", axis=3, tiled=True),
        lax.all_gather(kernel, "filt", axis=3, tiled=True),
    )
    nfilt = lax.axis_size("filt")
    ox = planes // 2
    oz = depth // 2
    oy_dev = rows // 2
    oy_all = rows * nfilt // 2
    row_id = lax.axis_index("filt")
    whole = lax.all_gather(volume, "filt", axis=1, tiled=True)
    lower = from_behind(whole[planes - 1 :], "space", 1)
    padded = jnp.pad(jnp.concatenate([lower, whole], axis=0), ((0, 0), (1, 1), (1, 1), (0, 0)))
    dims = (ox, oy_all, oz)
    features = (
        conv_out(padded, kernel, dims).reshape(ox, oy_all, oz, kernel.shape[3]).astype(jnp.bfloat16)
    )
    kgrad = weight_terms(padded, out_grad.reshape(-1, out_grad.shape[3]), dims)
    factor = float(ox * lax.axis_size("space") * oy_all * oz) ** (-0.5)
    kernel_grad = lax.psum(kgrad, "space") * factor
    grad_pad = jnp.pad(grad_all, ((0, 0), (0, 1), (0, 0), (0, 0)))
    window = lax.dynamic_slice_in_dim(grad_pad, row_id * oy_dev, oy_dev + 1, 1)
    scatter = parity_transpose(window, kern_all)
    face = scatter[0:1, 1 : rows + 1, 1 : depth + 1]
    above = from_behind(face, "space", -1)
    gradient = scatter[1 : planes + 1, 1 : rows + 1, 1 : depth + 1]
    gradient = gradient.at[planes - 1 :].add(above)
    return (features, gradient.astype(jnp.bfloat16), kernel_grad)


def solution(mesh):
    return jax.shard_map(
        on_device,
        mesh=mesh,
        in_specs=(
            P("space", "filt", None, None),
            P(None, None, None, "filt", None),
            P("space", None, None, "filt"),
        ),
        out_specs=(
            P("space", None, None, "filt"),
            P("space", "filt", None, None),
            P(None, None, None, "filt", None),
        ),
        check_vma=False,
    )
```

profile of v0, /device:TPU:7, one launch (start us, length us, event | category | flops | bytes accessed | tf_op | source)
XLA Modules:
  0.0 565.3 jit_solution(11206022533608373417)
XLA Ops:
  10.7 33.9 %all_gather.10 = bf16[1,64,16,256]{1,2,0,3:T(8,128)(2,1)S(1)} all-gather(bf16[1,64,16,32]{1,2,0,3:T(8,128)(2,1)S(1)} %copy.149), channel_id=1, replica_groups=mesh['space'=32,'filt'=8] {'filt'}, dimensions={3}, use_global_device_ids=true | all-gather | bytes 589824 | tf_op jit(solution)/shard_map/all_gather | solution.py:105
  47.0 24.1 %all-gather.5.cloned.1.call-done = bf16[3,3,3,256,128]{4,3,2,1,0:T(8,128)(2,1)} async-done(((bf16[3,3,3,32,128]{4,3,2,1,0:T(8,128)(2,1)}), bf16[3,3,3,256,128]{4,3,2,1,0:T(8,128)(2,1)}) %all-gather.5.cloned.1.call-update) | async-done | bytes 1769488 | tf_op jit(solution)/shard_map/all_gather | solution.py:106
  89.2 42.3 %all-gather.3.cloned.1.call-done = bf16[2,128,32,128]{3,1,2,0:T(8,128)(2,1)} async-done(((bf16[2,16,32,128]{3,1,2,0:T(8,128)(2,1)}), bf16[2,128,32,128]{3,1,2,0:T(8,128)(2,1)}) %all-gather.3.cloned.1.call-update) | async-done | bytes 2097168 | tf_op jit(solution)/shard_map/all_gather | solution.py:114
  143.1 6.3 %collective-permute-done.1 = f32[1,16,32,128]{3,0,2,1:T(1,128)S(1)} collective-permute-done((f32[1,16,32,128]{3,0,2,1:T(1,128)S(1)}, f32[1,16,32,128]{3,0,2,1:T(1,128)S(1)}, u32[]{:S(2)}, u32[]{:S(2)}) %collective-permute-start.1) | collective-permute-done | bytes 262176 | tf_op jit(solution)/shard_map/ppermute | solution.py:10
  149.8 5.8 %scatter-add.4 = bf16[2,16,32,128]{3,0,2,1:T(2,128)(2,1)S(1)} dynamic-update-slice(bf16[2,16,32,128]{3,0,2,1:T(2,128)(2,1)S(1)} %slice.500, bf16[1,16,32,128]{3,0,2,1:T(2,128)(2,1)S(1)} %slice_add_fusion, s32[]{:T(128)} %constant.40.clone.1, s32[]{:T(128)} %constant.36.clone.1, s32[]{:T(128)} %constant.36.clone.1, s32[]{:T(128)} %constant.36.clone.1) | dynamic-update-slice | bytes 262148 | tf_op jit(solution)/shard_map/scatter-add | solution.py:130
  160.0 5.5 slice.380
  165.5 5.0 slice.382
  170.5 5.0 slice.384
  190.4 5.0 slice.392
  200.3 5.0 slice.396
  215.2 5.0 slice.402
  230.1 5.0 slice.408
  235.1 5.0 slice.410
  240.1 5.0 slice.412
  245.1 5.0 slice.414
  255.0 5.0 slice.418
  260.0 7.1 %slice.420 = bf16[1,64,16,128]{3,1,2,0:T(8,128)(2,1)S(1)} slice(bf16[3,130,34,128]{3,1,2,0:T(8,128)(2,1)} %copy-done.1), slice={[2:3:1], [0:127:2], [2:33:2], [0:128:1]} | slice | bytes 524288 | tf_op jit(solution)/shard_map/slice | solution.py:16
  267.1 7.0 %slice.422 = bf16[1,64,16,128]{3,1,2,0:T(8,128)(2,1)S(1)} slice(bf16[3,130,34,128]{3,1,2,0:T(8,128)(2,1)} %copy-done.1), slice={[2:3:1], [1:128:2], [0:31:2], [0:128:1]} | slice | bytes 524288 | tf_op jit(solution)/shard_map/slice | solution.py:16
  274.1 7.1 %slice.424 = bf16[1,64,16,128]{3,1,2,0:T(8,128)(2,1)S(1)} slice(bf16[3,130,34,128]{3,1,2,0:T(8,128)(2,1)} %copy-done.1), slice={[2:3:1], [1:128:2], [1:32:2], [0:128:1]} | slice | bytes 524288 | tf_op jit(solution)/shard_map/slice | solution.py:16
  281.2 7.0 %slice.426 = bf16[1,64,16,128]{3,1,2,0:T(8,128)(2,1)S(1)} slice(bf16[3,130,34,128]{3,1,2,0:T(8,128)(2,1)} %copy-done.1), slice={[2:3:1], [1:128:2], [2:33:2], [0:128:1]} | slice | bytes 524288 | tf_op jit(solution)/shard_map/slice | solution.py:16
  288.2 7.4 %slice.428 = bf16[1,64,16,128]{3,1,2,0:T(8,128)(2,1)S(1)} slice(bf16[3,130,34,128]{3,1,2,0:T(8,128)(2,1)} %copy-done.1), slice={[2:3:1], [2:129:2], [0:31:2], [0:128:1]} | slice | bytes 524288 | tf_op jit(solution)/shard_map/slice | solution.py:16
  295.6 7.3 %slice.430 = bf16[1,64,16,128]{3,1,2,0:T(8,128)(2,1)S(1)} slice(bf16[3,130,34,128]{3,1,2,0:T(8,128)(2,1)} %copy-done.1), slice={[2:3:1], [2:129:2], [1:32:2], [0:128:1]} | slice | bytes 524288 | tf_op jit(solution)/shard_map/slice | solution.py:16
  303.0 7.4 %slice.432 = bf16[1,64,16,128]{3,1,2,0:T(8,128)(2,1)S(1)} slice(bf16[3,130,34,128]{3,1,2,0:T(8,128)(2,1)} %copy-done.1), slice={[2:3:1], [2:129:2], [2:33:2], [0:128:1]} | slice | bytes 524288 | tf_op jit(solution)/shard_map/slice | solution.py:16
  350.7 206.3 %all-reduce.5.cloned.1.call-done = f32[3,3,3,32,128]{4,3,2,1,0:T(8,128)} async-done(((f32[3,3,3,32,128]{4,3,2,1,0:T(8,128)}), f32[3,3,3,32,128]{4,3,2,1,0:T(8,128)}) %all-reduce.5.cloned.1.call-update) | async-done | bytes 442384 | tf_op jit(solution)/shard_map/psum | solution.py:123
  (261 shorter events, 126.2 us)
Async XLA Ops:
  7.2 63.8 %all-gather.5.cloned.1.call-start = ((), (), s32[]{:S(2)}) async-start(), calls=%async_computation.1 | async-start | bytes 1990656 | tf_op jit(solution)/shard_map/all_gather | solution.py:106
  7.9 123.6 %all-gather.3.cloned.1.call-start = ((), (), s32[]{:S(2)}) async-start(), calls=%async_computation | async-start | bytes 2359296 | tf_op jit(solution)/shard_map/all_gather | solution.py:114
  9.7 547.3 %all-reduce.5.cloned.1.call-start = ((), (), s32[]{:S(2)}) async-start(), calls=%async_computation.2 | async-start | bytes 884736 | tf_op jit(solution)/shard_map/psum | solution.py:123
  133.8 22.5 %collective-permute-start = (bf16[1,128,32,128]{3,1,2,0:T(8,128)(2,1)}, bf16[1,128,32,128]{3,1,2,0:T(8,128)(2,1)}, u32[]{:S(2)}, u32[]{:S(2)}) collective-permute-start(bf16[1,128,32,128]{3,1,2,0:T(8,128)(2,1)} %slice.472), channel_id=1, source_target_pairs={{0,8},{8,16},{16,24},{24,32},{32,40},{40,48},{48,56},{56,64},{64,7... | collective-permute-start | bytes 3145736 | tf_op jit(solution)/shard_map/ppermute | solution.py:10
  140.7 8.7 %collective-permute-start.1 = (f32[1,16,32,128]{3,0,2,1:T(1,128)S(1)}, f32[1,16,32,128]{3,0,2,1:T(1,128)S(1)}, u32[]{:S(2)}, u32[]{:S(2)}) collective-permute-start(f32[1,16,32,128]{3,0,2,1:T(1,128)S(1)} %slice.502), channel_id=1, source_target_pairs={{8,0},{16,8},{24,16},{32,24},{40,32},{48,40},{56,48},{64,56},{72,6... | collective-permute-start | bytes 786440 | tf_op jit(solution)/shard_map/ppermute | solution.py:10
  160.0 95.0 %copy-start.1 = (bf16[3,130,34,128]{3,1,2,0:T(8,128)(2,1)}, bf16[3,130,34,128]{3,1,2,0:T(8,128)(2,1)S(1)}, u32[]{:S(2)}) copy-start(bf16[3,130,34,128]{3,1,2,0:T(8,128)(2,1)S(1)} %fusion.6) | copy-start | bytes 10183684
  260.0 50.4 %copy-start = (bf16[1,64,16,32]{1,3,2,0:T(8,128)(2,1)S(1)}, bf16[1,64,16,32]{1,3,2,0:T(8,128)(2,1)}, u32[]{:S(2)}) copy-start(bf16[1,64,16,32]{1,3,2,0:T(8,128)(2,1)} %param.7) | copy-start | bytes 196612
  260.0 50.4 %copy-start.21 = (bf16[1,64,16,128]{3,1,2,0:T(8,128)(2,1)S(1)}, bf16[1,64,16,128]{3,1,2,0:T(8,128)(2,1)}, u32[]{:S(2)}) copy-start(bf16[1,64,16,128]{3,1,2,0:T(8,128)(2,1)} %slice.380) | copy-start | bytes 786436
  274.1 36.7 %copy-start.20 = (bf16[1,64,16,128]{3,1,2,0:T(8,128)(2,1)S(1)}, bf16[1,64,16,128]{3,1,2,0:T(8,128)(2,1)}, u32[]{:S(2)}) copy-start(bf16[1,64,16,128]{3,1,2,0:T(8,128)(2,1)} %slice.382) | copy-start | bytes 786436
  288.2 23.0 %copy-start.19 = (bf16[1,64,16,128]{3,1,2,0:T(8,128)(2,1)S(1)}, bf16[1,64,16,128]{3,1,2,0:T(8,128)(2,1)}, u32[]{:S(2)}) copy-start(bf16[1,64,16,128]{3,1,2,0:T(8,128)(2,1)} %slice.384) | copy-start | bytes 786436
  303.0 8.7 %copy-start.18 = (bf16[1,64,16,128]{3,1,2,0:T(8,128)(2,1)S(1)}, bf16[1,64,16,128]{3,1,2,0:T(8,128)(2,1)}, u32[]{:S(2)}) copy-start(bf16[1,64,16,128]{3,1,2,0:T(8,128)(2,1)} %slice.386) | copy-start | bytes 786436
  316.2 4.5 copy-start.8
  317.4 4.5 copy-start.7
  318.5 4.5 copy-start.6
  319.6 4.5 copy-start.5
  336.4 5.7 %copy-start.23 = (bf16[1,64,16,128]{3,2,1,0:T(8,128)(2,1)S(1)}, bf16[1,64,16,128]{3,2,1,0:T(8,128)(2,1)}, u32[]{:S(2)}) copy-start(bf16[1,64,16,128]{3,2,1,0:T(8,128)(2,1)} %copy.127) | copy-start | bytes 786436
  336.4 6.7 %copy-start.24 = (bf16[1,64,16,128]{3,2,1,0:T(8,128)(2,1)S(1)}, bf16[1,64,16,128]{3,2,1,0:T(8,128)(2,1)}, u32[]{:S(2)}) copy-start(bf16[1,64,16,128]{3,2,1,0:T(8,128)(2,1)} %copy.128) | copy-start | bytes 786436
  337.4 6.7 %copy-start.25 = (bf16[1,64,16,128]{3,2,1,0:T(8,128)(2,1)S(1)}, bf16[1,64,16,128]{3,2,1,0:T(8,128)(2,1)}, u32[]{:S(2)}) copy-start(bf16[1,64,16,128]{3,2,1,0:T(8,128)(2,1)} %copy.129) | copy-start | bytes 786436
  338.3 6.7 %copy-start.26 = (bf16[1,64,16,128]{3,2,1,0:T(8,128)(2,1)S(1)}, bf16[1,64,16,128]{3,2,1,0:T(8,128)(2,1)}, u32[]{:S(2)}) copy-start(bf16[1,64,16,128]{3,2,1,0:T(8,128)(2,1)} %copy.130) | copy-start | bytes 786436
  339.3 6.7 %copy-start.27 = (bf16[1,64,16,128]{3,2,1,0:T(8,128)(2,1)S(1)}, bf16[1,64,16,128]{3,2,1,0:T(8,128)(2,1)}, u32[]{:S(2)}) copy-start(bf16[1,64,16,128]{3,2,1,0:T(8,128)(2,1)} %copy.131) | copy-start | bytes 786436
  339.3 6.7 %copy-start.43 = (bf16[3,3,3,32,128]{4,3,2,1,0:T(8,128)(2,1)S(1)}, bf16[3,3,3,32,128]{4,3,2,1,0:T(8,128)(2,1)}, u32[]{:S(2)}) copy-start(bf16[3,3,3,32,128]{4,3,2,1,0:T(8,128)(2,1)} %param.6) | copy-start | bytes 663556
  340.2 6.0 %copy-start.28 = (bf16[1,64,16,128]{3,2,1,0:T(8,128)(2,1)S(1)}, bf16[1,64,16,128]{3,2,1,0:T(8,128)(2,1)}, u32[]{:S(2)}) copy-start(bf16[1,64,16,128]{3,2,1,0:T(8,128)(2,1)} %copy.132) | copy-start | bytes 786436
  341.2 5.2 copy-start.29
  342.2 4.5 copy-start.30
  (27 other events, 69.2 us)
Sparse Core Ops, SparseCore 0:
  10.5 60.4 all-gather.4
  74.1 57.4 all-gather.2
  336.6 220.3 all-reduce.4
where the time goes:
time: 571 us; the launch traced here: 565 us
  waiting for transfers between devices  280 us (49%)
  local copies, waits for them, and re-layouts  193 us (34%)
  blocking collectives  33.9 us (6%)
  matrix products  31.3 us (5%)
  between operations  15 us (3%)
  other arithmetic  7.26 us (1%)
  starting transfers between devices  5.75 us (1%)
    psum x1, waiting for transfers between devices, on_device(): kernel_grad = lax.psum(kgrad, 'space') * factor  206 us
    slice x54, local copies, waits for them, and re-layouts, take_patch(): lax.slice(padded, (a, b, c, 0), (a + 2 * ox - 1, b + 2 * oy - 1, c + 2 *...  169 us
    all_gather x1, waiting for transfers between devices, on_device(): whole = lax.all_gather(volume, 'filt', axis=1, tiled=True)  42.3 us
    all_gather x1, blocking collectives, on_device(): lax.all_gather(out_grad, 'filt', axis=3, tiled=True)  33.9 us
    all_gather x1, waiting for transfers between devices, on_device(): lax.all_gather(kernel, 'filt', axis=3, tiled=True)  24.1 us
    dot_general x27, matrix products, parity_transpose(): jnp.dot(window_piece, weights[a, b, c], preferred_element_type=jnp.float32)  13.4 us
    dot_general x27, matrix products, conv_out(): lax.dot_general(patch, weights[a, b, c], (((1,), (1,)), ((), ())), prefer...  12.2 us
  transfers between devices with their start and end apart: 5, of which 4 were waited for; matrix products, arithmetic and copies ran while one was open for 8% of the time, Pallas kernels for 0%

commit v1 on v0

v1 whole, which is shorter than its diff:
```python
import jax
import jax.numpy as jnp
from jax import lax
from jax.experimental import pallas as pl
from jax.experimental.pallas import tpu as pltpu
from jax.sharding import PartitionSpec as P

MESH = pl.DeviceIdType.MESH
F32 = jnp.float32
BF16 = jnp.bfloat16
NF = 8
NS = 32
NQ = 16
KS = [2 * t + e for e in range(2) for t in range(8)]

TAPS = {}
for _p in range(8):
    _x, _y, _z = _p // 4, (_p // 2) % 2, _p % 2
    TAPS[(0, _p)] = (1 + _x, 1 + _y, 1 + _z)
    if _z:
        TAPS[(1, _p)] = (1 + _x, 1 + _y, 0)
    if _x:
        TAPS[(2, _p)] = (0, 1 + _y, 1 + _z)
    if _y:
        TAPS[(3, _p)] = (1 + _x, 0, 1 + _z)
TAPS[(1, 4)] = (0, 1, 0)
TAPS[(1, 6)] = (0, 2, 0)
TAPS[(1, 0)] = (0, 0, 0)
TAPS[(2, 0)] = (0, 0, 1)
TAPS[(2, 1)] = (0, 0, 2)
TAPS[(3, 4)] = (1, 0, 0)
TAPS[(3, 0)] = (2, 0, 0)


def swap_blocks(arrs, unit):
    lane = lax.broadcasted_iota(jnp.int32, arrs[0].shape, 1)
    arrs = list(arrs)
    for bit in (4, 2, 1):
        step = bit * unit
        low = (lane & step) == 0
        for i in range(8):
            if i & bit:
                continue
            lo, hi = arrs[i], arrs[i | bit]
            arrs[i] = jnp.where(low, lo, pltpu.roll(hi, step, 1))
            arrs[i | bit] = jnp.where(low, pltpu.roll(lo, 128 - step, 1), hi)
    return arrs


def lane_blocks(shape, blocks):
    blk = lax.broadcasted_iota(jnp.int32, shape, 1) >> 4
    hit = blk == blocks[0]
    for b in blocks[1:]:
        hit = hit | (blk == b)
    return hit


def shift_row(w):
    row = lax.broadcasted_iota(jnp.int32, w.shape, 0)
    first = (row & 7) == 0
    prev = jnp.where(row < 128, 0.0, pltpu.roll(w, 121, 0))
    return jnp.where(first, prev, pltpu.roll(w, 1, 0))


def shift_depth(w):
    w = w.reshape(8, 16, 8, 128)
    even, odd = w[:, :8], w[:, 8:]
    back = jnp.concatenate([jnp.zeros_like(odd[:, :1]), odd[:, :7]], axis=1)
    return jnp.concatenate([back, even], axis=1).reshape(1024, 128)


def four_shifts(w_bf16):
    w = w_bf16.astype(F32).reshape(1024, 128)
    wj = shift_row(w)
    return [w.astype(BF16), shift_depth(w).astype(BF16), wj.astype(BF16), shift_depth(wj).astype(BF16)]


def selection(dj, dk):
    m = lax.broadcasted_iota(jnp.int32, (128, 256), 0)
    n = lax.broadcasted_iota(jnp.int32, (128, 256), 1)
    row = (m & 7) + dj
    k = 2 * ((m >> 3) & 7) + (m >> 6) + dk
    lane = (row >> 3) * 128 + (k & 1) * 64 + (k >> 1) * 8 + (row & 7)
    return jnp.where((n == lane) & (k < 16), 1.0, 0.0).astype(BF16)


def dot_t(x, y):
    return lax.dot_general(x, y, (((1,), (1,)), ((), ())), preferred_element_type=F32)


def body(
    vol, ker, grad, feat_out, ig_out, kg_out,
    vf, halo_b, halo_r, halo_c, vs, wbuf, gs, gtb, gnext, kall, rhs, rt, s1, asum, s2, own3, kb, fs, fb, pb, gv, igf,
    snd_g, rcv_g, snd_v, rcv_v, snd_k, rcv_k, snd_h, rcv_h, snd_m, rcv_m, snd_2, rcv_2, snd_3, rcv_3, snd_f, rcv_f,
):
    s = lax.axis_index("space")
    f = lax.axis_index("filt")
    core = s % 2
    q = s // 2
    sib = s + 1 - 2 * core
    sx = s + 2 - 4 * (q % 2)
    up = (s + 1) % NS
    down = (s + NS - 1) % NS
    fup = (f + 1) % NF
    fdown = (f + NF - 1) % NF
    fx = f + 1 - 2 * (f % 2)
    dest = q // 2
    half = q % 2

    barrier = pltpu.get_barrier_semaphore()
    hello = [(s, (f + i) % NF) for i in range(1, NF)]
    hello += [(sx, (fx + 2 * i) % NF) for i in range(4)]
    hello += [(sib, f), (down, f), (up, f), (down, fdown)]
    hello += [(2 * ((q + i) % NQ) + core, f) for i in range(1, NQ)]
    hello += [(2 * (2 * f + r) + core, (f + i) % NF) for r in range(2) for i in range(NF)]
    for dev in hello:
        pl.semaphore_signal(barrier, inc=1, device_id=dev, device_id_type=MESH)

    sent = []

    def copy(src, dst, ss, rs, dev):
        c = pltpu.make_async_remote_copy(
            src_ref=src, dst_ref=dst, send_sem=ss, recv_sem=rs, device_id=dev, device_id_type=MESH
        )
        return c

    def send(*args):
        c = copy(*args)
        c.start()
        sent.append(c)

    def arrived(dst, ss, rs):
        copy(dst, dst, ss, rs, (sib, f)).wait_recv()

    for px in range(2):
        vf[pl.ds(((1 + px) * 17 + 1) * 32, 512), :] = vol[px].astype(F32).reshape(512, 128)
    parity = []
    for p in range(8):
        a, b, z = 1 + p // 4, 1 + (p // 2) % 2, p % 2
        parity.append(
            jnp.concatenate([vf[pl.ds((a * 17 + b) * 32 + 2 * k + z, 8, stride=64), :] for k in KS], axis=0)
        )
    for i, x in enumerate(swap_blocks(parity, 16)):
        vs[i] = x.astype(BF16)
    tiles = [
        jnp.concatenate([grad[2 * t].astype(F32), grad[2 * t + 1].astype(F32)], axis=1) for t in range(8)
    ]
    for i, x in enumerate(swap_blocks(tiles, 8)):
        gs[i] = x.astype(BF16)

    pl.semaphore_wait(barrier, len(hello))

    for i in range(1, NF):
        to = (f + i) % NF
        send(gs, gtb.at[:, f], snd_g.at[i - 1], rcv_g.at[i - 1], (s, to))
    for i in range(1, NF):
        to = (f + i) % NF
        send(vs.at[to], wbuf.at[0, f], snd_v.at[i - 1], rcv_v.at[i - 1], (s, to))
    for i in range(1, 4):
        send(ker.at[:, core], kall.at[:, f, core], snd_k.at[i - 1], rcv_k.at[i - 1], (s, (f + 2 * i) % NF))
    for i in range(4):
        send(ker.at[:, core], kall.at[:, f, core], snd_k.at[3 + i], rcv_k.at[3 + i], (sx, (fx + 2 * i) % NF))
    send(vol.at[1], halo_b, snd_h.at[0], rcv_h.at[0], (up, f))
    send(vol.at[:, 15], halo_r, snd_h.at[1], rcv_h.at[1], (s, fup))
    send(vol.at[1, 15], halo_c, snd_h.at[2], rcv_h.at[2], (up, fup))

    wbuf[0, f] = vs[f]
    gtb[:, f] = gs[...]
    kall[:, f, core] = ker[:, core]

    for i in range(1, NF):
        arrived(wbuf.at[0, (f + NF - i) % NF], snd_v.at[i - 1], rcv_v.at[i - 1])
    send(wbuf.at[0], wbuf.at[1], snd_m.at[0], rcv_m.at[0], (up, f))
    for i, x in enumerate(four_shifts(wbuf[0])):
        rhs[:, i * 128 : i * 128 + 128] = x
    for i in range(1, NF):
        arrived(gtb.at[:, (f + NF - i) % NF], snd_g.at[i - 1], rcv_g.at[i - 1])
    send(gtb.at[f], gnext.at[0], snd_m.at[1], rcv_m.at[1], (down, f))
    send(gtb.at[fup], gnext.at[1], snd_m.at[2], rcv_m.at[2], (down, f))
    gall = jnp.concatenate([gtb[t].reshape(256, 128) for t in range(8)], axis=1)
    own = jnp.dot(gall, rhs[...], preferred_element_type=F32)

    arrived(wbuf.at[1], snd_m.at[0], rcv_m.at[0])
    for i, x in enumerate(four_shifts(wbuf[1])):
        rhs[:, i * 128 : i * 128 + 128] = jnp.where(s > 0, x, jnp.zeros_like(x))
    below = jnp.dot(gall, rhs[...], preferred_element_type=F32)
    o = [own[:, i * 128 : i * 128 + 128] for i in range(4)]
    b = [below[:, i * 128 : i * 128 + 128] for i in range(4)]
    shape = (256, 128)
    rt[0] = o[0]
    x = jnp.where(lane_blocks(shape, (4, 6)), pltpu.roll(b[1], 112, 1), o[1])
    rt[1] = jnp.where(lane_blocks(shape, (0,)), pltpu.roll(b[3], 16, 1), x)
    rt[2] = jnp.where(lane_blocks(shape, (0, 1)), pltpu.roll(b[2], 32, 1), b[0])
    rt[3] = jnp.where(lane_blocks(shape, (0, 4)), pltpu.roll(o[3], 16, 1), o[2])

    send(rt.at[pl.ds(2 * (1 - core), 2)], s1, snd_m.at[3], rcv_m.at[3], (sib, f))
    for i in range(1, 4):
        arrived(kall.at[:, (f + NF - 2 * i) % NF, core], snd_k.at[i - 1], rcv_k.at[i - 1])
    for i in range(4):
        arrived(kall.at[:, (fx + NF - 2 * i) % NF, core], snd_k.at[3 + i], rcv_k.at[3 + i])
    send(kall.at[:, :, core], kall.at[:, :, core], snd_m.at[4], rcv_m.at[4], (sib, f))
    arrived(s1, snd_m.at[3], rcv_m.at[3])
    for l in range(2):
        asum[l] = (rt[2 * core + l] + s1[l]).reshape(16, 16, 128)
    for i in range(1, NQ):
        qd = (q + i) % NQ
        send(asum.at[:, qd], s2.at[i - 1], snd_2.at[i - 1], rcv_2.at[i - 1], (2 * qd + core, f))

    arrived(halo_b, snd_h.at[0], rcv_h.at[0])
    arrived(halo_r, snd_h.at[1], rcv_h.at[1])
    arrived(halo_c, snd_h.at[2], rcv_h.at[2])
    low = halo_b[...].astype(F32).reshape(512, 128)
    vf[pl.ds(32, 512), :] = jnp.where(s > 0, low, jnp.zeros_like(low))
    edge = halo_c[...].astype(F32)
    vf[pl.ds(0, 32), :] = jnp.where((s > 0) & (f > 0), edge, jnp.zeros_like(edge))
    for px in range(2):
        edge = halo_r[px].astype(F32)
        vf[pl.ds((1 + px) * 17 * 32, 32), :] = jnp.where(f > 0, edge, jnp.zeros_like(edge))
    for a in range(3):
        for b3 in range(3):
            def cells(z):
                return vf[pl.ds((a * 17 + b3) * 32 + z, 8, stride=64), :]
            for c in range(3):
                col = ((a * 3 + b3) * 3 + c) * 128
                rows = [
                    jnp.zeros((8, 128), F32) if 2 * k + c == 0 else cells(2 * k + c - 1) for k in KS
                ]
                pb[:, col : col + 128] = jnp.concatenate(rows, axis=0).astype(BF16)
    arrived(kall.at[:, :, 1 - core], snd_m.at[4], rcv_m.at[4])
    total = jnp.zeros((256, 128), F32)
    for a in range(3):
        taps = jnp.concatenate([kall[9 * a + n].reshape(256, 128) for n in range(9)], axis=1)
        total = total + dot_t(taps, pb[:, 1152 * a : 1152 * a + 1152])
    fs[...] = total.astype(BF16).reshape(8, 32, 128)
    for i in range(1, NF):
        to = (f + i) % NF
        send(fs.at[to], fb.at[f], snd_f.at[i - 1], rcv_f.at[i - 1], (s, to))
    fb[f] = fs[f]

    for i in range(1, NQ):
        arrived(s2.at[i - 1], snd_2.at[i - 1], rcv_2.at[i - 1])
    acc = asum[:, q]
    for i in range(1, NQ):
        acc = acc + s2[i - 1]
    own3[...] = acc
    slot = kb.at[f, pl.ds(2 * core, 2), half]
    for i in range(1, NQ):
        qd = (q + i) % NQ
        send(own3, slot, snd_3.at[i], rcv_3.at[8 * half + f], (2 * qd + core, dest))
    home = copy(own3, slot, snd_3.at[0], rcv_3.at[8 * half + f], (s, dest))

    @pl.when(f != dest)
    def _():
        home.start()

    @pl.when(f == dest)
    def _():
        kb[f, pl.ds(2 * core, 2), half] = own3[...]

    arrived(gnext.at[0], snd_m.at[1], rcv_m.at[1])
    arrived(gnext.at[1], snd_m.at[2], rcv_m.at[2])
    picks = jnp.concatenate([selection(dj, dk) for dj in range(2) for dk in range(2)], axis=0)
    here = gtb[f].reshape(256, 128)
    nxt = gtb[fup].reshape(256, 128)
    nxt = jnp.where(f < NF - 1, nxt, jnp.zeros_like(nxt))
    gv[0] = dot_t(picks, jnp.concatenate([here, nxt], axis=1)).astype(BF16)
    here = gnext[0].reshape(256, 128)
    here = jnp.where(s < NS - 1, here, jnp.zeros_like(here))
    nxt = gnext[1].reshape(256, 128)
    nxt = jnp.where((s < NS - 1) & (f < NF - 1), nxt, jnp.zeros_like(nxt))
    gv[1] = dot_t(picks, jnp.concatenate([here, nxt], axis=1)).astype(BF16)
    steps = (((1, 0),), ((0, 1), (2, 0)))
    for px in range(2):
        for py in range(2):
            for pz in range(2):
                left, right = [], []
                for a, di in steps[px]:
                    for b3, dj in steps[py]:
                        for c, dk in steps[pz]:
                            v = (2 * dj + dk) * 128
                            left.append(gv[di, v : v + 128])
                            right.append(kall[9 * a + 3 * b3 + c].reshape(256, 128))
                res = jnp.dot(
                    jnp.concatenate(left, axis=1), jnp.concatenate(right, axis=0), preferred_element_type=F32
                )
                for n, k in enumerate(KS):
                    igf[pl.ds((px * 16 + py) * 32 + 2 * k + pz, 8, stride=64), :] = res[8 * n : 8 * n + 8]
    ig_out[...] = igf[...].reshape(2, 16, 32, 128).astype(BF16)

    for r in range(2):
        for i in range(NF):
            src = (f + i) % NF
            got = copy(
                own3, kb.at[src, pl.ds(2 * core, 2), r], snd_3.at[0], rcv_3.at[8 * r + src], (sib, f)
            )
            if i == 0:
                @pl.when(2 * f + r != q)
                def _():
                    got.wait_recv()
            else:
                got.wait_recv()
    send(kb.at[:, pl.ds(2 * core, 2)], kb.at[:, pl.ds(2 * core, 2)], snd_m.at[5], rcv_m.at[5], (sib, f))

    for i in range(1, NF):
        arrived(fb.at[(f + NF - i) % NF], snd_f.at[i - 1], rcv_f.at[i - 1])
    for t, x in enumerate(swap_blocks([fb[i].astype(F32) for i in range(8)], 8)):
        feat_out[2 * t] = x[:, :64].astype(BF16)
        feat_out[2 * t + 1] = x[:, 64:].astype(BF16)

    arrived(kb.at[:, pl.ds(2 * (1 - core), 2)], snd_m.at[5], rcv_m.at[5])
    factor = float(32 * 64 * 16) ** -0.5
    for lt in range(4):
        blocks = swap_blocks([kb[i, lt].reshape(32, 128) for i in range(8)], 16)
        for pos in range(8):
            if (lt, pos) in TAPS:
                a, b3, c = TAPS[(lt, pos)]
                kg_out[9 * a + 3 * b3 + c] = blocks[pos] * factor

    for c in sent:
        c.wait_send()

    @pl.when(f != dest)
    def _():
        home.wait_send()


def on_device(volume, kernel, out_grad):
    vmem = pl.BlockSpec(memory_space=pltpu.VMEM)
    dma = pltpu.SemaphoreType.DMA
    feat, ig, kg = pl.pallas_call(
        body,
        out_shape=(
            jax.ShapeDtypeStruct((16, 32, 64), BF16),
            jax.ShapeDtypeStruct((2, 16, 32, 128), BF16),
            jax.ShapeDtypeStruct((27, 32, 128), F32),
        ),
        in_specs=[vmem] * 3,
        out_specs=(vmem,) * 3,
        scratch_shapes=[
            pltpu.VMEM((3 * 17 * 32, 128), F32),
            pltpu.VMEM((16, 32, 128), BF16),
            pltpu.VMEM((2, 32, 128), BF16),
            pltpu.VMEM((32, 128), BF16),
            pltpu.VMEM((8, 128, 128), BF16),
            pltpu.VMEM((2, 8, 128, 128), BF16),
            pltpu.VMEM((8, 32, 128), BF16),
            pltpu.VMEM((8, 8, 32, 128), BF16),
            pltpu.VMEM((2, 8, 32, 128), BF16),
            pltpu.VMEM((27, 8, 2, 16, 128), BF16),
            pltpu.VMEM((1024, 512), BF16),
            pltpu.VMEM((4, 256, 128), F32),
            pltpu.VMEM((2, 256, 128), F32),
            pltpu.VMEM((2, 16, 16, 128), F32),
            pltpu.VMEM((15, 2, 16, 128), F32),
            pltpu.VMEM((2, 16, 128), F32),
            pltpu.VMEM((8, 4, 2, 16, 128), F32),
            pltpu.VMEM((8, 32, 128), BF16),
            pltpu.VMEM((8, 32, 128), BF16),
            pltpu.VMEM((128, 27 * 128), BF16),
            pltpu.VMEM((2, 512, 256), BF16),
            pltpu.VMEM((2 * 16 * 32, 128), F32),
            dma((7,)), dma((7,)), dma((7,)), dma((7,)), dma((7,)), dma((7,)),
            dma((3,)), dma((3,)), dma((6,)), dma((6,)), dma((15,)), dma((15,)),
            dma((16,)), dma((16,)), dma((7,)), dma((7,)),
        ],
        compiler_params=pltpu.CompilerParams(
            collective_id=0, has_side_effects=True, vmem_limit_bytes=48 * 1024 * 1024
        ),
        name="conv_fwd_bwd",
    )(volume, kernel.reshape(27, 2, 16, 128), out_grad.transpose(0, 2, 3, 1).reshape(16, 32, 64))
    features = feat.reshape(1, 16, 32, 64).transpose(0, 3, 1, 2)
    return features, ig, kg.reshape(3, 3, 3, 32, 128)


def solution(mesh):
    return jax.shard_map(
        on_device,
        mesh=mesh,
        in_specs=(
            P("space", "filt", None, None),
            P(None, None, None, "filt", None),
            P("space", None, None, "filt"),
        ),
        out_specs=(
            P("space", None, None, "filt"),
            P("space", "filt", None, None),
            P(None, None, None, "filt", None),
        ),
        check_vma=False,
    )
```

time: 571 us -> 58.7 us (0.10)
  waiting for transfers between devices: 280 us -> 0 us
  local copies, waits for them, and re-layouts: 193 us -> 4.9 us
  Pallas kernels: 0 us -> 53 us
  blocking collectives: 33.9 us -> 0 us
  matrix products: 31.3 us -> 0 us
  between operations: 15 us -> 0.65 us
  other arithmetic: 7.26 us -> 0 us
  starting transfers between devices: 5.75 us -> 0 us
    psum x1 -> x0, waiting for transfers between devices: 206 us -> none  [on_device(): kernel_grad = lax.psum(kgrad, 'space') * factor]
    slice x58 -> x0, local copies, waits for them, and re-layouts: 172 us -> none  [the longest x54 169 us: take_patch(): lax.slice(padded, (a, b, c, 0), (a + 2 * ox - 1, b + 2 * oy - 1, c + 2 *...]
    all_gather x2 -> x0, waiting for transfers between devices: 66.3 us -> none  [the longest x1 42.3 us: on_device(): whole = lax.all_gather(volume, 'filt', axis=1, tiled=True)]
    pallas_call x0 -> x1, Pallas kernels: none -> 53 us  [on_device(): pl.pallas_call(body, out_shape=(jax.ShapeDtypeStruct((16, 32, 64), BF16),...]
    all_gather x1 -> x0, blocking collectives: 33.9 us -> none  [on_device(): lax.all_gather(out_grad, 'filt', axis=3, tiled=True)]
    dot_general x81 -> x0, matrix products: 31.3 us -> none  [the longest x27 13.4 us: parity_transpose(): jnp.dot(window_piece, weights[a, b, c], preferred_element_type=jnp.float32)]
    ppermute x2 -> x0, waiting for transfers between devices: 6.28 us -> none  [from_behind(): return lax.ppermute(shard, axis, pairs)]
    another operation x14 -> x0, local copies, waits for them, and re-layouts: 6.27 us -> none  [the longest x11 5.46 us: parity_transpose(): jnp.stack(depth_list, axis=3)]
  transfers between devices with their start and end apart: 5 -> 0, of which waited for: 4 -> 0; matrix products, arithmetic and copies ran while one was open for 8% -> 0% of each run, Pallas kernels for 0% -> 0%
where the time goes in v1:
time: 58.7 us; the launch traced here: 58.5 us
  Pallas kernels  53 us (90%)
  local copies, waits for them, and re-layouts  4.9 us (8%)
  between operations  0.65 us (1%)
    pallas_call x1, Pallas kernels, on_device(): pl.pallas_call(body, out_shape=(jax.ShapeDtypeStruct((16, 32, 64), BF16),...  53 us
    unnamed x9, local copies, waits for them, and re-layouts  4.9 us

profile of v1, /device:TPU:7, one launch (start us, length us, event | category | flops | bytes accessed | tf_op | source)
XLA Modules:
  0.0 58.5 jit_solution(14193828926240484420)
XLA Ops:
  0.6 0.0 copy-start
  0.6 0.9 %copy-done = bf16[2,16,32,128]{3,2,1,0:T(8,128)(2,1)S(1)} copy-done((bf16[2,16,32,128]{3,2,1,0:T(8,128)(2,1)S(1)}, bf16[2,16,32,128]{3,2,1,0:T(8,128)(2,1)}, u32[]{:S(2)}) %copy-start) | copy-done | bytes 262168
  1.6 0.0 copy-start.1
  1.6 0.9 %copy-done.1 = bf16[3,3,3,32,128]{4,3,2,1,0:T(8,128)(2,1)S(1)} copy-done((bf16[3,3,3,32,128]{4,3,2,1,0:T(8,128)(2,1)S(1)}, bf16[3,3,3,32,128]{4,3,2,1,0:T(8,128)(2,1)}, u32[]{:S(2)}) %copy-start.1) | copy-done | bytes 221208
  2.5 0.0 copy-start.2
  2.5 0.9 %copy-done.2 = bf16[1,64,16,32]{1,3,2,0:T(8,128)(2,1)S(1)} copy-done((bf16[1,64,16,32]{1,3,2,0:T(8,128)(2,1)S(1)}, bf16[1,64,16,32]{1,3,2,0:T(8,128)(2,1)}, u32[]{:S(2)}) %copy-start.2) | copy-done | bytes 65560
  3.4 53.0 %conv_fwd_bwd.1 = (bf16[16,32,64]{2,1,0:T(8,128)(2,1)S(1)}, bf16[2,16,32,128]{3,2,1,0:T(8,128)(2,1)S(1)}, f32[27,32,128]{2,1,0:T(8,128)S(1)}) custom-call(bf16[2,16,32,128]{3,2,1,0:T(8,128)(2,1)S(1)} %copy-done, bf16[27,2,16,128]{3,2,1,0:T(8,128)(2,1)S(1)} %bitcast.9, bf16[16,32,64]{2,1,0:T(8,128)(2,1)S(1)} %bitcast.10), custom_call_target="tpu_custom_call" | custom-call | tf_op jit(solution)/shard_map/conv_fwd_bwd/pallas_call | solution.py:330
  56.4 0.7 %copy.9 = bf16[1,64,16,32]{1,3,2,0:T(8,128)(2,1)} copy(bf16[1,64,16,32]{1,3,2,0:T(8,128)(2,1)S(1)} %bitcast.11) | data formatting | bytes 131072
  57.1 0.7 %copy.10 = bf16[2,16,32,128]{3,2,1,0:T(8,128)(2,1)} copy(bf16[2,16,32,128]{3,2,1,0:T(8,128)(2,1)S(1)} %get-tuple-element.13) | data formatting | bytes 524288
  57.8 0.8 %copy.11 = f32[3,3,3,32,128]{4,3,2,1,0:T(8,128)} copy(f32[3,3,3,32,128]{4,3,2,1,0:T(8,128)S(1)} %bitcast.8) | data formatting | bytes 884736
Async XLA Ops:
  0.6 1.0 %copy-start = (bf16[2,16,32,128]{3,2,1,0:T(8,128)(2,1)S(1)}, bf16[2,16,32,128]{3,2,1,0:T(8,128)(2,1)}, u32[]{:S(2)}) copy-start(bf16[2,16,32,128]{3,2,1,0:T(8,128)(2,1)} %vol.1) | copy-start | bytes 786436
  1.6 0.9 %copy-start.1 = (bf16[3,3,3,32,128]{4,3,2,1,0:T(8,128)(2,1)S(1)}, bf16[3,3,3,32,128]{4,3,2,1,0:T(8,128)(2,1)}, u32[]{:S(2)}) copy-start(bf16[3,3,3,32,128]{4,3,2,1,0:T(8,128)(2,1)} %param.4) | copy-start | bytes 663556
  2.5 0.9 %copy-start.2 = (bf16[1,64,16,32]{1,3,2,0:T(8,128)(2,1)S(1)}, bf16[1,64,16,32]{1,3,2,0:T(8,128)(2,1)}, u32[]{:S(2)}) copy-start(bf16[1,64,16,32]{1,3,2,0:T(8,128)(2,1)} %param.5) | copy-start | bytes 196612

commit v2 on v1

v2 whole, which is shorter than its diff:
```python
import jax
import jax.numpy as jnp
from jax import lax
from jax.experimental import pallas as pl
from jax.experimental.pallas import tpu as pltpu
from jax.sharding import PartitionSpec as P

MESH = pl.DeviceIdType.MESH
F32 = jnp.float32
BF16 = jnp.bfloat16
NF = 8
NS = 32
NQ = 16
KS = [2 * t + e for e in range(2) for t in range(8)]

TAPS = {}
for _p in range(8):
    _x, _y, _z = _p // 4, (_p // 2) % 2, _p % 2
    TAPS[(0, _p)] = (1 + _x, 1 + _y, 1 + _z)
    if _z:
        TAPS[(1, _p)] = (1 + _x, 1 + _y, 0)
    if _x:
        TAPS[(2, _p)] = (0, 1 + _y, 1 + _z)
    if _y:
        TAPS[(3, _p)] = (1 + _x, 0, 1 + _z)
TAPS[(1, 4)] = (0, 1, 0)
TAPS[(1, 6)] = (0, 2, 0)
TAPS[(1, 0)] = (0, 0, 0)
TAPS[(2, 0)] = (0, 0, 1)
TAPS[(2, 1)] = (0, 0, 2)
TAPS[(3, 4)] = (1, 0, 0)
TAPS[(3, 0)] = (2, 0, 0)


def swap_blocks(arrs, unit):
    lane = lax.broadcasted_iota(jnp.int32, arrs[0].shape, 1)
    arrs = list(arrs)
    for bit in (4, 2, 1):
        step = bit * unit
        low = (lane & step) == 0
        for i in range(8):
            if i & bit:
                continue
            lo, hi = arrs[i], arrs[i | bit]
            arrs[i] = jnp.where(low, lo, pltpu.roll(hi, step, 1))
            arrs[i | bit] = jnp.where(low, pltpu.roll(lo, 128 - step, 1), hi)
    return arrs


def lane_blocks(shape, blocks):
    blk = lax.broadcasted_iota(jnp.int32, shape, 1) >> 4
    hit = blk == blocks[0]
    for b in blocks[1:]:
        hit = hit | (blk == b)
    return hit


def shift_row(w):
    row = lax.broadcasted_iota(jnp.int32, w.shape, 0)
    first = (row & 7) == 0
    prev = jnp.where(row < 128, 0.0, pltpu.roll(w, 121, 0))
    return jnp.where(first, prev, pltpu.roll(w, 1, 0))


def shift_depth(w):
    w = w.reshape(8, 16, 8, 128)
    even, odd = w[:, :8], w[:, 8:]
    back = jnp.concatenate([jnp.zeros_like(odd[:, :1]), odd[:, :7]], axis=1)
    return jnp.concatenate([back, even], axis=1).reshape(1024, 128)


def four_shifts(w_bf16):
    w = w_bf16.astype(F32).reshape(1024, 128)
    wj = shift_row(w)
    return [w.astype(BF16), shift_depth(w).astype(BF16), wj.astype(BF16), shift_depth(wj).astype(BF16)]


def selection(dj, dk):
    m = lax.broadcasted_iota(jnp.int32, (128, 256), 0)
    n = lax.broadcasted_iota(jnp.int32, (128, 256), 1)
    row = (m & 7) + dj
    k = 2 * ((m >> 3) & 7) + (m >> 6) + dk
    lane = (row >> 3) * 128 + (k & 1) * 64 + (k >> 1) * 8 + (row & 7)
    return jnp.where((n == lane) & (k < 16), 1.0, 0.0).astype(BF16)


def dot_t(x, y):
    return lax.dot_general(x, y, (((1,), (1,)), ((), ())), preferred_element_type=F32)


def body(
    vol_hbm, ker_hbm, grad_hbm, feat_out, ig_out, kg_out,
    vol, grad, vf, halo_b, halo_r, halo_c, vs, wbuf, gs, gtb, gnext, kall, rhs, rt, s1, asum, s2, own3, kb, fs, fb,
    pb, gv, igf,
    ins, snd_g, rcv_g, snd_v, rcv_v, snd_k, rcv_k, snd_h, rcv_h, snd_m, rcv_m, snd_2, rcv_2, snd_3, rcv_3,
    snd_f, rcv_f,
):
    s = lax.axis_index("space")
    f = lax.axis_index("filt")
    core = s % 2
    q = s // 2
    sib = s + 1 - 2 * core
    up = (s + 1) % NS
    down = (s + NS - 1) % NS
    fup = (f + 1) % NF
    fdown = (f + NF - 1) % NF
    dest = q // 2
    half = q % 2

    get_vol = pltpu.make_async_copy(vol_hbm, vol, ins.at[0])
    get_grad = pltpu.make_async_copy(grad_hbm, grad, ins.at[1])
    get_ker = pltpu.make_async_copy(ker_hbm.at[:, core], kall.at[f, core], ins.at[2])
    get_vol.start()
    get_grad.start()
    get_ker.start()

    barrier = pltpu.get_barrier_semaphore()
    hello = [(s, (f + i) % NF) for i in range(1, NF)]
    hello += [(sib, f), (down, f), (up, f), (down, fdown)]
    hello += [(2 * ((q + i) % NQ) + core, f) for i in range(1, NQ)]
    hello += [(2 * (2 * f + r) + core, (f + i) % NF) for r in range(2) for i in range(NF)]
    for dev in hello:
        pl.semaphore_signal(barrier, inc=1, device_id=dev, device_id_type=MESH)

    sent = []

    def copy(src, dst, ss, rs, dev):
        return pltpu.make_async_remote_copy(
            src_ref=src, dst_ref=dst, send_sem=ss, recv_sem=rs, device_id=dev, device_id_type=MESH
        )

    def send(*args):
        c = copy(*args)
        c.start()
        sent.append(c)

    def arrived(dst, ss, rs):
        copy(dst, dst, ss, rs, (sib, f)).wait_recv()

    get_vol.wait()
    for px in range(2):
        vf[pl.ds(((1 + px) * 17 + 1) * 32, 512), :] = vol[px].astype(F32).reshape(512, 128)
    parity = []
    for p in range(8):
        a, b, z = 1 + p // 4, 1 + (p // 2) % 2, p % 2
        parity.append(
            jnp.concatenate([vf[pl.ds((a * 17 + b) * 32 + 2 * k + z, 8, stride=64), :] for k in KS], axis=0)
        )
    for i, x in enumerate(swap_blocks(parity, 16)):
        vs[i] = x.astype(BF16)
    get_grad.wait()
    tiles = [
        jnp.concatenate([grad[2 * t].astype(F32), grad[2 * t + 1].astype(F32)], axis=1) for t in range(8)
    ]
    for i, x in enumerate(swap_blocks(tiles, 8)):
        gs[i] = x.astype(BF16)

    pl.semaphore_wait(barrier, len(hello))

    for i in range(1, NF):
        to = (f + i) % NF
        send(vs.at[to], wbuf.at[0, f], snd_v.at[i - 1], rcv_v.at[i - 1], (s, to))
    for i in range(1, NF):
        to = (f + i) % NF
        send(gs, gtb.at[f], snd_g.at[i - 1], rcv_g.at[i - 1], (s, to))
    wbuf[0, f] = vs[f]
    gtb[f] = gs[...]

    for i in range(1, NF):
        arrived(wbuf.at[0, (f + NF - i) % NF], snd_v.at[i - 1], rcv_v.at[i - 1])
    send(wbuf.at[0], wbuf.at[1], snd_m.at[0], rcv_m.at[0], (up, f))
    for i, x in enumerate(four_shifts(wbuf[0])):
        rhs[:, i * 128 : i * 128 + 128] = x
    for i in range(1, NF):
        arrived(gtb.at[(f + NF - i) % NF], snd_g.at[i - 1], rcv_g.at[i - 1])
    get_ker.wait()
    for i in range(1, NF):
        send(kall.at[f, core], kall.at[f, core], snd_k.at[i - 1], rcv_k.at[i - 1], (s, (f + i) % NF))
    gall = jnp.concatenate([gtb[:, t].reshape(256, 128) for t in range(8)], axis=1)
    own = jnp.dot(gall, rhs[...], preferred_element_type=F32)
    o = [own[:, i * 128 : i * 128 + 128] for i in range(4)]
    shape = (256, 128)
    rt[0] = o[0]
    rt[3] = jnp.where(lane_blocks(shape, (0, 4)), pltpu.roll(o[3], 16, 1), o[2])
    send(rt.at[3 * (1 - core)], s1.at[0], snd_m.at[3], rcv_m.at[3], (sib, f))
    send(vol.at[1], halo_b, snd_h.at[0], rcv_h.at[0], (up, f))
    send(vol.at[:, 15], halo_r, snd_h.at[1], rcv_h.at[1], (s, fup))
    send(vol.at[1, 15], halo_c, snd_h.at[2], rcv_h.at[2], (up, fup))
    send(gtb.at[:, f], gnext.at[0], snd_m.at[1], rcv_m.at[1], (down, f))
    send(gtb.at[:, fup], gnext.at[1], snd_m.at[2], rcv_m.at[2], (down, f))

    arrived(wbuf.at[1], snd_m.at[0], rcv_m.at[0])
    for i, x in enumerate(four_shifts(wbuf[1])):
        rhs[:, i * 128 : i * 128 + 128] = jnp.where(s > 0, x, jnp.zeros_like(x))
    below = jnp.dot(gall, rhs[...], preferred_element_type=F32)
    b = [below[:, i * 128 : i * 128 + 128] for i in range(4)]
    x = jnp.where(lane_blocks(shape, (4, 6)), pltpu.roll(b[1], 112, 1), o[1])
    rt[1] = jnp.where(lane_blocks(shape, (0,)), pltpu.roll(b[3], 16, 1), x)
    rt[2] = jnp.where(lane_blocks(shape, (0, 1)), pltpu.roll(b[2], 32, 1), b[0])
    send(rt.at[2 - core], s1.at[1], snd_m.at[4], rcv_m.at[4], (sib, f))

    for l in range(2):
        arrived(s1.at[l], snd_m.at[3 + l], rcv_m.at[3 + l])
        kept = 3 * core if l == 0 else 1 + core
        asum[l] = (rt[kept] + s1[l]).reshape(16, 16, 128)
        for i in range(1, NQ):
            qd = (q + i) % NQ
            n = 15 * l + i - 1
            send(asum.at[l, qd], s2.at[l, i - 1], snd_2.at[n], rcv_2.at[n], (2 * qd + core, f))

    homes = []
    for l in range(2):
        for i in range(1, NQ):
            n = 15 * l + i - 1
            arrived(s2.at[l, i - 1], snd_2.at[n], rcv_2.at[n])
        acc = asum[l, q]
        for i in range(1, NQ):
            acc = acc + s2[l, i - 1]
        own3[l] = acc
        kept = 3 * core if l == 0 else 1 + core
        slot = kb.at[f, kept, half]
        got = rcv_3.at[16 * l + 8 * half + f]
        for i in range(1, NQ):
            qd = (q + i) % NQ
            send(own3.at[l], slot, snd_3.at[16 * l + i], got, (2 * qd + core, dest))
        homes.append(copy(own3.at[l], slot, snd_3.at[16 * l], got, (s, dest)))

        @pl.when(f != dest)
        def _():
            homes[l].start()

        @pl.when(f == dest)
        def _():
            kb[f, kept, half] = own3[l]

    for i in range(1, NF):
        arrived(kall.at[(f + NF - i) % NF, core], snd_k.at[i - 1], rcv_k.at[i - 1])
    send(kall.at[:, core], kall.at[:, core], snd_m.at[5], rcv_m.at[5], (sib, f))

    arrived(halo_b, snd_h.at[0], rcv_h.at[0])
    arrived(halo_r, snd_h.at[1], rcv_h.at[1])
    arrived(halo_c, snd_h.at[2], rcv_h.at[2])
    low = halo_b[...].astype(F32).reshape(512, 128)
    vf[pl.ds(32, 512), :] = jnp.where(s > 0, low, jnp.zeros_like(low))
    edge = halo_c[...].astype(F32)
    vf[pl.ds(0, 32), :] = jnp.where((s > 0) & (f > 0), edge, jnp.zeros_like(edge))
    for px in range(2):
        edge = halo_r[px].astype(F32)
        vf[pl.ds((1 + px) * 17 * 32, 32), :] = jnp.where(f > 0, edge, jnp.zeros_like(edge))
    for a in range(3):
        for b3 in range(3):
            def cells(z):
                return vf[pl.ds((a * 17 + b3) * 32 + z, 8, stride=64), :]
            for c in range(3):
                col = ((a * 3 + b3) * 3 + c) * 128
                rows = [
                    jnp.zeros((8, 128), F32) if 2 * k + c == 0 else cells(2 * k + c - 1) for k in KS
                ]
                pb[:, col : col + 128] = jnp.concatenate(rows, axis=0).astype(BF16)

    def tap(n):
        return kall[:, :, n].reshape(256, 128)

    arrived(kall.at[:, 1 - core], snd_m.at[5], rcv_m.at[5])
    total = jnp.zeros((256, 128), F32)
    for a in range(3):
        taps = jnp.concatenate([tap(9 * a + n) for n in range(9)], axis=1)
        total = total + dot_t(taps, pb[:, 1152 * a : 1152 * a + 1152])
    fs[...] = total.astype(BF16).reshape(8, 32, 128)
    for i in range(1, NF):
        to = (f + i) % NF
        send(fs.at[to], fb.at[f], snd_f.at[i - 1], rcv_f.at[i - 1], (s, to))
    fb[f] = fs[f]

    arrived(gnext.at[0], snd_m.at[1], rcv_m.at[1])
    arrived(gnext.at[1], snd_m.at[2], rcv_m.at[2])
    picks = jnp.concatenate([selection(dj, dk) for dj in range(2) for dk in range(2)], axis=0)
    here = gtb[:, f].reshape(256, 128)
    nxt = gtb[:, fup].reshape(256, 128)
    nxt = jnp.where(f < NF - 1, nxt, jnp.zeros_like(nxt))
    gv[0] = dot_t(picks, jnp.concatenate([here, nxt], axis=1)).astype(BF16)
    here = gnext[0].reshape(256, 128)
    here = jnp.where(s < NS - 1, here, jnp.zeros_like(here))
    nxt = gnext[1].reshape(256, 128)
    nxt = jnp.where((s < NS - 1) & (f < NF - 1), nxt, jnp.zeros_like(nxt))
    gv[1] = dot_t(picks, jnp.concatenate([here, nxt], axis=1)).astype(BF16)
    steps = (((1, 0),), ((0, 1), (2, 0)))
    for px in range(2):
        for py in range(2):
            for pz in range(2):
                left, right = [], []
                for a, di in steps[px]:
                    for b3, dj in steps[py]:
                        for c, dk in steps[pz]:
                            v = (2 * dj + dk) * 128
                            left.append(gv[di, v : v + 128])
                            right.append(tap(9 * a + 3 * b3 + c))
                res = jnp.dot(
                    jnp.concatenate(left, axis=1), jnp.concatenate(right, axis=0), preferred_element_type=F32
                )
                for n, k in enumerate(KS):
                    igf[pl.ds((px * 16 + py) * 32 + 2 * k + pz, 8, stride=64), :] = res[8 * n : 8 * n + 8]
    ig_out[...] = igf[...].reshape(2, 16, 32, 128).astype(BF16)

    for l in range(2):
        kept = 3 * core if l == 0 else 1 + core
        for r in range(2):
            for i in range(NF):
                src = (f + i) % NF
                got = copy(
                    own3.at[l], kb.at[src, kept, r], snd_3.at[0], rcv_3.at[16 * l + 8 * r + src], (sib, f)
                )
                if i == 0:
                    @pl.when(2 * f + r != q)
                    def _():
                        got.wait_recv()
                else:
                    got.wait_recv()
        send(kb.at[:, kept], kb.at[:, kept], snd_m.at[6 + l], rcv_m.at[6 + l], (sib, f))

    for i in range(1, NF):
        arrived(fb.at[(f + NF - i) % NF], snd_f.at[i - 1], rcv_f.at[i - 1])
    for t, x in enumerate(swap_blocks([fb[i].astype(F32) for i in range(8)], 8)):
        feat_out[2 * t] = x[:, :64].astype(BF16)
        feat_out[2 * t + 1] = x[:, 64:].astype(BF16)

    factor = float(32 * 64 * 16) ** -0.5
    for l in range(2):
        arrived(kb.at[:, 3 * (1 - core) if l == 0 else 2 - core], snd_m.at[6 + l], rcv_m.at[6 + l])
        for lt in ((0, 3), (1, 2))[l]:
            blocks = swap_blocks([kb[i, lt].reshape(32, 128) for i in range(8)], 16)
            for pos in range(8):
                if (lt, pos) in TAPS:
                    a, b3, c = TAPS[(lt, pos)]
                    kg_out[9 * a + 3 * b3 + c] = blocks[pos] * factor

    for c in sent:
        c.wait_send()
    for c in homes:
        @pl.when(f != dest)
        def _():
            c.wait_send()


def on_device(volume, kernel, out_grad):
    vmem = pl.BlockSpec(memory_space=pltpu.VMEM)
    hbm = pl.BlockSpec(memory_space=pltpu.HBM)
    dma = pltpu.SemaphoreType.DMA
    inputs = (volume, kernel.reshape(27, 2, 16, 128), out_grad.transpose(0, 2, 3, 1).reshape(16, 32, 64))
    feat, ig, kg = pl.pallas_call(
        body,
        out_shape=(
            jax.ShapeDtypeStruct((16, 32, 64), BF16),
            jax.ShapeDtypeStruct((2, 16, 32, 128), BF16),
            jax.ShapeDtypeStruct((27, 32, 128), F32),
        ),
        in_specs=[hbm] * 3,
        out_specs=(vmem,) * 3,
        scratch_shapes=[
            pltpu.VMEM((2, 16, 32, 128), BF16),
            pltpu.VMEM((16, 32, 64), BF16),
            pltpu.VMEM((3 * 17 * 32, 128), F32),
            pltpu.VMEM((16, 32, 128), BF16),
            pltpu.VMEM((2, 32, 128), BF16),
            pltpu.VMEM((32, 128), BF16),
            pltpu.VMEM((8, 128, 128), BF16),
            pltpu.VMEM((2, 8, 128, 128), BF16),
            pltpu.VMEM((8, 32, 128), BF16),
            pltpu.VMEM((8, 8, 32, 128), BF16),
            pltpu.VMEM((2, 8, 32, 128), BF16),
            pltpu.VMEM((8, 2, 27, 16, 128), BF16),
            pltpu.VMEM((1024, 512), BF16),
            pltpu.VMEM((4, 256, 128), F32),
            pltpu.VMEM((2, 256, 128), F32),
            pltpu.VMEM((2, 16, 16, 128), F32),
            pltpu.VMEM((2, 15, 16, 128), F32),
            pltpu.VMEM((2, 16, 128), F32),
            pltpu.VMEM((8, 4, 2, 16, 128), F32),
            pltpu.VMEM((8, 32, 128), BF16),
            pltpu.VMEM((8, 32, 128), BF16),
            pltpu.VMEM((128, 27 * 128), BF16),
            pltpu.VMEM((2, 512, 256), BF16),
            pltpu.VMEM((2 * 16 * 32, 128), F32),
            dma((3,)),
            dma((7,)), dma((7,)), dma((7,)), dma((7,)), dma((7,)), dma((7,)),
            dma((3,)), dma((3,)), dma((8,)), dma((8,)), dma((30,)), dma((30,)),
            dma((32,)), dma((32,)), dma((7,)), dma((7,)),
        ],
        compiler_params=pltpu.CompilerParams(
            collective_id=0, has_side_effects=True, vmem_limit_bytes=40 * 1024 * 1024
        ),
        name="conv_fwd_bwd",
    )(*[pltpu.with_memory_space_constraint(x, pltpu.HBM) for x in inputs])
    features = feat.reshape(1, 16, 32, 64).transpose(0, 3, 1, 2)
    return features, ig, kg.reshape(3, 3, 3, 32, 128)


def solution(mesh):
    return jax.shard_map(
        on_device,
        mesh=mesh,
        in_specs=(
            P("space", "filt", None, None),
            P(None, None, None, "filt", None),
            P("space", None, None, "filt"),
        ),
        out_specs=(
            P("space", None, None, "filt"),
            P("space", "filt", None, None),
            P(None, None, None, "filt", None),
        ),
        check_vma=False,
    )
```

time: 58.7 us -> 54.9 us (0.935)
  local copies, waits for them, and re-layouts: 4.9 us -> 2.12 us
  Pallas kernels: 53 us -> 51.6 us
    unnamed x9 -> x3, local copies, waits for them, and re-layouts: 4.9 us -> 2.12 us
    pallas_call x1, Pallas kernels: 53 us -> 51.6 us  [on_device(): pl.pallas_call(body, out_shape=(jax.ShapeDtypeStruct((16, 32, 64), BF16),...]
where the time goes in v2:
time: 54.9 us; the launch traced here: 54.3 us
  Pallas kernels  51.6 us (94%)
  local copies, waits for them, and re-layouts  2.12 us (4%)
  between operations  0.64 us (1%)
    pallas_call x1, Pallas kernels, on_device(): pl.pallas_call(body, out_shape=(jax.ShapeDtypeStruct((16, 32, 64), BF16),...  51.6 us
    unnamed x3, local copies, waits for them, and re-layouts  2.12 us

profile of v2, /device:TPU:7, one launch (start us, length us, event | category | flops | bytes accessed | tf_op | source)
XLA Modules:
  0.0 54.3 jit_solution(1678540210175237167)
XLA Ops:
  0.6 51.6 %conv_fwd_bwd.1 = (bf16[16,32,64]{2,1,0:T(8,128)(2,1)S(1)}, bf16[2,16,32,128]{3,2,1,0:T(8,128)(2,1)S(1)}, f32[27,32,128]{2,1,0:T(8,128)S(1)}) custom-call(bf16[2,16,32,128]{3,2,1,0:T(8,128)(2,1)} %vol_hbm.1, bf16[27,2,16,128]{3,2,1,0:T(8,128)(2,1)} %bitcast.10, bf16[16,32,64]{2,1,0:T(8,128)(2,1)} %bitcast.11), custom_call_target="tpu_custom_call" | custom-call | tf_op jit(solution)/shard_map/conv_fwd_bwd/pallas_call | solution.py:350
  52.2 0.7 %copy.9 = bf16[1,64,16,32]{1,3,2,0:T(8,128)(2,1)} copy(bf16[1,64,16,32]{1,3,2,0:T(8,128)(2,1)S(1)} %bitcast.9) | data formatting | bytes 131072
  52.8 0.7 %copy.10 = bf16[2,16,32,128]{3,2,1,0:T(8,128)(2,1)} copy(bf16[2,16,32,128]{3,2,1,0:T(8,128)(2,1)S(1)} %get-tuple-element.13) | data formatting | bytes 524288
  53.5 0.8 %copy.11 = f32[3,3,3,32,128]{4,3,2,1,0:T(8,128)} copy(f32[3,3,3,32,128]{4,3,2,1,0:T(8,128)S(1)} %bitcast.8) | data formatting | bytes 884736

commit v3 on v2

--- a/solution.py
+++ b/solution.py
@@ -11,6 +11,7 @@
 NF = 8
 NS = 32
 NQ = 16
+FAR = (8, 7, 9, 6, 10, 5, 11, 4, 12, 3, 13, 2, 14, 1, 15)
 KS = [2 * t + e for e in range(2) for t in range(8)]
 
 TAPS = {}
@@ -100,6 +101,8 @@
     core = s % 2
     q = s // 2
     sib = s + 1 - 2 * core
+    sx = s + 2 - 4 * (q % 2)
+    fx = f + 1 - 2 * (f % 2)
     up = (s + 1) % NS
     down = (s + NS - 1) % NS
     fup = (f + 1) % NF
@@ -116,7 +119,7 @@
 
     barrier = pltpu.get_barrier_semaphore()
     hello = [(s, (f + i) % NF) for i in range(1, NF)]
-    hello += [(sib, f), (down, f), (up, f), (down, fdown)]
+    hello += [(sx, fx), (sib, f), (down, f), (up, f), (down, fdown)]
     hello += [(2 * ((q + i) % NQ) + core, f) for i in range(1, NQ)]
     hello += [(2 * (2 * f + r) + core, (f + i) % NF) for r in range(2) for i in range(NF)]
     for dev in hello:
@@ -157,25 +160,35 @@
 
     pl.semaphore_wait(barrier, len(hello))
 
+    send(gs, gtb.at[f], snd_g.at[0], rcv_g.at[0], (s, fx))
     for i in range(1, NF):
         to = (f + i) % NF
         send(vs.at[to], wbuf.at[0, f], snd_v.at[i - 1], rcv_v.at[i - 1], (s, to))
-    for i in range(1, NF):
-        to = (f + i) % NF
-        send(gs, gtb.at[f], snd_g.at[i - 1], rcv_g.at[i - 1], (s, to))
+    for i in range(1, 4):
+        send(gs, gtb.at[f], snd_g.at[i], rcv_g.at[i], (s, (f + 2 * i) % NF))
     wbuf[0, f] = vs[f]
     gtb[f] = gs[...]
+
+    get_ker.wait()
+    send(kall.at[f, core], kall.at[f, core], snd_k.at[0], rcv_k.at[0], (sx, fx))
+    arrived(gtb.at[fx], snd_g.at[0], rcv_g.at[0])
+    for i in range(1, 4):
+        send(gtb.at[fx], gtb.at[fx], snd_g.at[3 + i], rcv_g.at[3 + i], (s, (f + 2 * i) % NF))
 
     for i in range(1, NF):
         arrived(wbuf.at[0, (f + NF - i) % NF], snd_v.at[i - 1], rcv_v.at[i - 1])
     send(wbuf.at[0], wbuf.at[1], snd_m.at[0], rcv_m.at[0], (up, f))
     for i, x in enumerate(four_shifts(wbuf[0])):
         rhs[:, i * 128 : i * 128 + 128] = x
-    for i in range(1, NF):
-        arrived(gtb.at[(f + NF - i) % NF], snd_g.at[i - 1], rcv_g.at[i - 1])
-    get_ker.wait()
-    for i in range(1, NF):
-        send(kall.at[f, core], kall.at[f, core], snd_k.at[i - 1], rcv_k.at[i - 1], (s, (f + i) % NF))
+    for i in range(1, 4):
+        arrived(gtb.at[(f + NF - 2 * i) % NF], snd_g.at[i], rcv_g.at[i])
+    for i in range(1, 4):
+        arrived(gtb.at[(fx + NF - 2 * i) % NF], snd_g.at[3 + i], rcv_g.at[3 + i])
+    arrived(kall.at[fx, core], snd_k.at[0], rcv_k.at[0])
+    for n, by in enumerate((2, 6)):
+        to = (s, (f + by) % NF)
+        send(kall.at[f, core], kall.at[f, core], snd_k.at[1 + n], rcv_k.at[1 + n], to)
+        send(kall.at[fx, core], kall.at[fx, core], snd_k.at[3 + n], rcv_k.at[3 + n], to)
     gall = jnp.concatenate([gtb[:, t].reshape(256, 128) for t in range(8)], axis=1)
     own = jnp.dot(gall, rhs[...], preferred_element_type=F32)
     o = [own[:, i * 128 : i * 128 + 128] for i in range(4)]
@@ -203,10 +216,15 @@
         arrived(s1.at[l], snd_m.at[3 + l], rcv_m.at[3 + l])
         kept = 3 * core if l == 0 else 1 + core
         asum[l] = (rt[kept] + s1[l]).reshape(16, 16, 128)
-        for i in range(1, NQ):
+        for i in FAR:
             qd = (q + i) % NQ
             n = 15 * l + i - 1
             send(asum.at[l, qd], s2.at[l, i - 1], snd_2.at[n], rcv_2.at[n], (2 * qd + core, f))
+
+    arrived(kall.at[(f + 6) % NF, core], snd_k.at[1], rcv_k.at[1])
+    send(kall.at[(f + 6) % NF, core], kall.at[(f + 6) % NF, core], snd_k.at[5], rcv_k.at[5], (s, (f + 2) % NF))
+    arrived(kall.at[(fx + 2) % NF, core], snd_k.at[4], rcv_k.at[4])
+    send(kall.at[(fx + 2) % NF, core], kall.at[(fx + 2) % NF, core], snd_k.at[6], rcv_k.at[6], (s, (f + 6) % NF))
 
     homes = []
     for l in range(2):
@@ -220,7 +238,7 @@
         kept = 3 * core if l == 0 else 1 + core
         slot = kb.at[f, kept, half]
         got = rcv_3.at[16 * l + 8 * half + f]
-        for i in range(1, NQ):
+        for i in FAR:
             qd = (q + i) % NQ
             send(own3.at[l], slot, snd_3.at[16 * l + i], got, (2 * qd + core, dest))
         homes.append(copy(own3.at[l], slot, snd_3.at[16 * l], got, (s, dest)))
@@ -233,8 +251,10 @@
         def _():
             kb[f, kept, half] = own3[l]
 
-    for i in range(1, NF):
-        arrived(kall.at[(f + NF - i) % NF, core], snd_k.at[i - 1], rcv_k.at[i - 1])
+    arrived(kall.at[(f + 2) % NF, core], snd_k.at[2], rcv_k.at[2])
+    arrived(kall.at[(fx + 6) % NF, core], snd_k.at[3], rcv_k.at[3])
+    arrived(kall.at[(f + 4) % NF, core], snd_k.at[5], rcv_k.at[5])
+    arrived(kall.at[(fx + 4) % NF, core], snd_k.at[6], rcv_k.at[6])
     send(kall.at[:, core], kall.at[:, core], snd_m.at[5], rcv_m.at[5], (sib, f))
 
     arrived(halo_b, snd_h.at[0], rcv_h.at[0])

time: 54.9 us -> 46.5 us (0.85)
  Pallas kernels: 51.6 us -> 43.5 us
    pallas_call x1, Pallas kernels: 51.6 us -> 43.5 us  [on_device(): pl.pallas_call(body, out_shape=(jax.ShapeDtypeStruct((16, 32, 64), BF16),...]
where the time goes in v3:
time: 46.5 us; the launch traced here: 46.3 us
  Pallas kernels  43.5 us (94%)
  local copies, waits for them, and re-layouts  2.12 us (5%)
  between operations  0.64 us (1%)
    pallas_call x1, Pallas kernels, on_device(): pl.pallas_call(body, out_shape=(jax.ShapeDtypeStruct((16, 32, 64), BF16),...  43.5 us
    unnamed x3, local copies, waits for them, and re-layouts  2.12 us

profile of v3, /device:TPU:7, one launch (start us, length us, event | category | flops | bytes accessed | tf_op | source)
XLA Modules:
  0.0 46.3 jit_solution(1754842886666737736)
XLA Ops:
  0.6 43.5 %conv_fwd_bwd.1 = (bf16[16,32,64]{2,1,0:T(8,128)(2,1)S(1)}, bf16[2,16,32,128]{3,2,1,0:T(8,128)(2,1)S(1)}, f32[27,32,128]{2,1,0:T(8,128)S(1)}) custom-call(bf16[2,16,32,128]{3,2,1,0:T(8,128)(2,1)} %vol_hbm.1, bf16[27,2,16,128]{3,2,1,0:T(8,128)(2,1)} %bitcast.10, bf16[16,32,64]{2,1,0:T(8,128)(2,1)} %bitcast.11), custom_call_target="tpu_custom_call" | custom-call | tf_op jit(solution)/shard_map/conv_fwd_bwd/pallas_call | solution.py:370
  44.1 0.7 %copy.9 = bf16[1,64,16,32]{1,3,2,0:T(8,128)(2,1)} copy(bf16[1,64,16,32]{1,3,2,0:T(8,128)(2,1)S(1)} %bitcast.9) | data formatting | bytes 131072
  44.8 0.7 %copy.10 = bf16[2,16,32,128]{3,2,1,0:T(8,128)(2,1)} copy(bf16[2,16,32,128]{3,2,1,0:T(8,128)(2,1)S(1)} %get-tuple-element.13) | data formatting | bytes 524288
  45.5 0.8 %copy.11 = f32[3,3,3,32,128]{4,3,2,1,0:T(8,128)} copy(f32[3,3,3,32,128]{4,3,2,1,0:T(8,128)S(1)} %bitcast.8) | data formatting | bytes 884736

commit v4 on v3

--- a/solution.py
+++ b/solution.py
@@ -320,7 +320,7 @@
                 )
                 for n, k in enumerate(KS):
                     igf[pl.ds((px * 16 + py) * 32 + 2 * k + pz, 8, stride=64), :] = res[8 * n : 8 * n + 8]
-    ig_out[...] = igf[...].reshape(2, 16, 32, 128).astype(BF16)
+    ig_out[...] = igf[: 2 * 16 * 32].reshape(2, 16, 32, 128).astype(BF16)
 
     for l in range(2):
         kept = 3 * core if l == 0 else 1 + core
@@ -379,7 +379,7 @@
         scratch_shapes=[
             pltpu.VMEM((2, 16, 32, 128), BF16),
             pltpu.VMEM((16, 32, 64), BF16),
-            pltpu.VMEM((3 * 17 * 32, 128), F32),
+            pltpu.VMEM((3 * 17 * 32 + 64, 128), F32),
             pltpu.VMEM((16, 32, 128), BF16),
             pltpu.VMEM((2, 32, 128), BF16),
             pltpu.VMEM((32, 128), BF16),
@@ -400,7 +400,7 @@
             pltpu.VMEM((8, 32, 128), BF16),
             pltpu.VMEM((128, 27 * 128), BF16),
             pltpu.VMEM((2, 512, 256), BF16),
-            pltpu.VMEM((2 * 16 * 32, 128), F32),
+            pltpu.VMEM((2 * 16 * 32 + 64, 128), F32),
             dma((3,)),
             dma((7,)), dma((7,)), dma((7,)), dma((7,)), dma((7,)), dma((7,)),
             dma((3,)), dma((3,)), dma((8,)), dma((8,)), dma((30,)), dma((30,)),

time: 46.5 us -> 46.5 us (level)
  no operation moved by 1% of the time
where the time goes in v4:
time: 46.5 us; the launch traced here: 46.3 us
  Pallas kernels  43.5 us (94%)
  local copies, waits for them, and re-layouts  2.12 us (5%)
  between operations  0.64 us (1%)
    pallas_call x1, Pallas kernels, on_device(): pl.pallas_call(body, out_shape=(jax.ShapeDtypeStruct((16, 32, 64), BF16),...  43.5 us
    unnamed x3, local copies, waits for them, and re-layouts  2.12 us

profile of v4, /device:TPU:7, one launch (start us, length us, event | category | flops | bytes accessed | tf_op | source)
XLA Modules:
  0.0 46.3 jit_solution(11668884512013667713)
XLA Ops:
  0.6 43.5 %conv_fwd_bwd.1 = (bf16[16,32,64]{2,1,0:T(8,128)(2,1)S(1)}, bf16[2,16,32,128]{3,2,1,0:T(8,128)(2,1)S(1)}, f32[27,32,128]{2,1,0:T(8,128)S(1)}) custom-call(bf16[2,16,32,128]{3,2,1,0:T(8,128)(2,1)} %vol_hbm.1, bf16[27,2,16,128]{3,2,1,0:T(8,128)(2,1)} %bitcast.10, bf16[16,32,64]{2,1,0:T(8,128)(2,1)} %bitcast.11), custom_call_target="tpu_custom_call" | custom-call | tf_op jit(solution)/shard_map/conv_fwd_bwd/pallas_call | solution.py:370
  44.1 0.7 %copy.9 = bf16[1,64,16,32]{1,3,2,0:T(8,128)(2,1)} copy(bf16[1,64,16,32]{1,3,2,0:T(8,128)(2,1)S(1)} %bitcast.9) | data formatting | bytes 131072
  44.8 0.7 %copy.10 = bf16[2,16,32,128]{3,2,1,0:T(8,128)(2,1)} copy(bf16[2,16,32,128]{3,2,1,0:T(8,128)(2,1)S(1)} %get-tuple-element.13) | data formatting | bytes 524288
  45.5 0.8 %copy.11 = f32[3,3,3,32,128]{4,3,2,1,0:T(8,128)} copy(f32[3,3,3,32,128]{4,3,2,1,0:T(8,128)S(1)} %bitcast.8) | data formatting | bytes 884736
